TPU v7x, 32 devices: a whole 2x2x4 slice. The times are simulated.
32 devices in a mesh: grp: 4 (over z), seq: 8 (over y, x, core).
Axes of the slice: x: 2, y: 2, z: 4, core: 2. Of those that a mesh axis runs over, the one named last changes fastest.
Arguments:
- fine_rows: bfloat16 [4, 1024, 2048], P('grp', 'seq'), may hold values from -6 to 6
- segment_ids: int32 [4, 1024], P('grp', 'seq'), may hold values from 0 to 7, as said below
- pool_gain: float32 [2048], replicated, may hold values from 0.1 to 1.9
- w_in: bfloat16 [2048, 8192], P('grp', 'seq'), may hold values from -0.125 to 0.125
- w_gate: bfloat16 [8192, 16384], P('grp', 'seq'), may hold values from -0.0625 to 0.0625
- w_up: bfloat16 [8192, 16384], P('grp', 'seq'), may hold values from -0.0625 to 0.0625
- w_down: bfloat16 [16384, 8192], P('seq', 'grp'), may hold values from -0.046875 to 0.046875
- out_grad: bfloat16 [4, 64, 8192], P('grp'), may hold values from -6 to 6
Outputs:
- coarse_out: bfloat16 [4, 64, 8192], P('grp', None, 'seq')
- fine_grad: bfloat16 [4, 1024, 2048], P('grp', 'seq')
Inputs may be any that keep to these rules, and one draw needn't show every extreme that they name: `segment_ids`: within each shard of 128 consecutive bytes the numbers count the shard's segments from 0 upward, never falling, every segment one byte or more; a shard holds 4 to 8 segments, some shard of every document exactly 8, and every document 48 segments in all.
All inputs are finite; a program needn't handle non-finite values.
Results may differ from a plain program's by a relative error of at most 0.02.
Values may be sent and summed in bfloat16 or wider, within the bound.
A program may use at most 192 MiB of HBM per device.

v0:
```python
import jax
import jax.numpy as jnp
from jax import lax
from jax.sharding import PartitionSpec as P

SEG_CAP = 8
norm_eps = 1e-06
bf16 = jnp.bfloat16
f32 = jnp.float32


def silu_parts(gate_value):
    sigma = jax.nn.sigmoid(gate_value)
    return (gate_value * sigma, sigma * (1.0 + gate_value * (1.0 - sigma)))


def matmul(a, b):
    return jnp.dot(a, b, preferred_element_type=f32)


def matmul_t(a, b):
    return lax.dot_general(a, b, (((1,), (1,)), ((), ())), preferred_element_type=f32)


def swap_pairs(grps, seqs):
    halves = seqs // grps
    return [
        (g * seqs + p * halves + h, p * seqs + g * halves + h)
        for g in range(grps)
        for p in range(grps)
        for h in range(halves)
    ]


def grp_total(partial_value):
    return lax.psum_scatter(
        partial_value.astype(bf16), "grp", scatter_dimension=0, tiled=True
    ).astype(f32)


def make_shards(grps, seqs):
    halves = seqs // grps
    pairs = swap_pairs(grps, seqs)

    def swap(value):
        return lax.ppermute(value, ("grp", "seq"), pairs)

    def shards(fine_rows, segment_ids, pool_gain, w_in, w_gate, w_up, w_down, out_grad):
        rows_here = fine_rows[0]
        index_here = segment_ids[0]
        feat, width = w_in.shape
        slots = jnp.arange(SEG_CAP, dtype=jnp.int32)
        member = index_here[None, :] == slots[:, None]
        segment_sums = matmul(member.astype(bf16), rows_here)
        inv_rms = lax.rsqrt(jnp.mean(segment_sums * segment_sums, axis=1, keepdims=True) + norm_eps)
        pooled = (segment_sums * inv_rms * pool_gain).astype(bf16)
        live_count = jnp.max(index_here) + 1
        packed = jnp.concatenate(
            [pooled, jnp.full((1, pooled.shape[1]), live_count.astype(bf16))], axis=0
        )
        gathered = lax.all_gather(packed, "seq", axis=0)
        shard_counts = gathered[:, SEG_CAP, 0].astype(jnp.int32)
        gathered = gathered[:, :SEG_CAP].reshape(seqs * SEG_CAP, -1)
        offsets = jnp.cumsum(shard_counts) - shard_counts
        slot_count = seqs * SEG_CAP
        within = jnp.tile(slots, seqs)
        target = jnp.repeat(offsets, SEG_CAP) + within
        is_live = within < jnp.repeat(shard_counts, SEG_CAP)
        rows = slot_count * 3 // 4
        select = (target[None, :] == jnp.arange(rows, dtype=jnp.int32)[:, None]) & is_live[None, :]
        selector = select.astype(bf16)
        work_in = matmul(selector, gathered).astype(bf16)
        work_in = lax.all_to_all(
            work_in.reshape(rows, grps, feat), "grp", split_axis=1, concat_axis=0
        ).reshape(grps * rows, feat)
        x_cols = grp_total(matmul(work_in, w_in)).astype(bf16)
        seq_at = lax.axis_index("seq")
        block = w_gate.shape[0]
        piece = block // seqs
        grad_here = out_grad[0].reshape(slot_count, grps, seqs, piece)
        grad_part = lax.dynamic_index_in_dim(grad_here, seq_at, 2, keepdims=False)
        grad_part = matmul(selector, grad_part.reshape(slot_count, grps * piece)).astype(bf16)
        grad_part = lax.all_to_all(
            grad_part.reshape(rows, grps, piece), "grp", split_axis=1, concat_axis=0
        ).reshape(grps * rows, piece)
        work_grad = lax.all_gather(grad_part, "seq", axis=1, tiled=True)
        grad_hidden = grp_total(matmul_t(work_grad, w_down))

        def spread(cols):
            every = lax.all_gather(swap(cols), "seq", axis=0)
            every = every.reshape(grps, halves, rows, width)
            return every.transpose(0, 2, 1, 3).reshape(grps * rows, halves * width)

        def column_total(part):
            part = part.astype(bf16).reshape(grps, rows, halves, width)
            part = part.transpose(0, 2, 1, 3).reshape(seqs * rows, width)
            return swap(lax.psum_scatter(part, "seq", scatter_dimension=0, tiled=True)).astype(f32)

        coarse_x = spread(x_cols)
        gate_value = grp_total(matmul(coarse_x, w_gate))
        up_value = grp_total(matmul(coarse_x, w_up))
        activated, derivative = silu_parts(gate_value)
        hidden = (activated * up_value).astype(bf16)
        grad_gate = (grad_hidden * up_value * derivative).astype(bf16)
        grad_up = (grad_hidden * activated).astype(bf16)
        grad_gate = lax.all_gather(grad_gate, "grp", axis=0, tiled=True)
        grad_up = lax.all_gather(grad_up, "grp", axis=0, tiled=True)
        hidden = lax.all_gather(hidden, "grp", axis=0, tiled=True)
        back_cols = column_total(matmul_t(grad_gate, w_gate) + matmul_t(grad_up, w_up))
        down_cols = column_total(matmul(hidden, w_down))
        out_cols = (x_cols.astype(f32) + down_cols).astype(bf16)
        out_cols = matmul(selector.T, out_cols).astype(bf16)
        grad_cols = lax.dynamic_slice_in_dim(out_grad[0], seq_at * width, width, 1)
        grad_cols = matmul(selector, grad_cols)
        grad_x = (back_cols + grad_cols).astype(bf16)
        grad_x = lax.all_gather(grad_x, "grp", axis=0, tiled=True)
        term = matmul_t(grad_x, w_in).astype(bf16)
        term = lax.all_to_all(
            term.reshape(grps, rows, feat), "grp", split_axis=0, concat_axis=1
        ).reshape(rows, grps * feat)
        term = matmul(selector.T, term).astype(bf16)
        grad_pooled = lax.psum_scatter(term, "seq", scatter_dimension=0, tiled=True).astype(f32)
        weighted = grad_pooled * pool_gain
        inner = jnp.mean(weighted * segment_sums, axis=1, keepdims=True)
        grad_sums = inv_rms * weighted - segment_sums * (inv_rms * inv_rms * inv_rms) * inner
        fine_grad = matmul(member.astype(bf16).T, grad_sums.astype(bf16)).astype(bf16)
        return (out_cols[None], fine_grad[None])

    return shards


def solution(mesh):
    return jax.shard_map(
        make_shards(mesh.shape["grp"], mesh.shape["seq"]),
        mesh=mesh,
        in_specs=(
            P("grp", "seq", None),
            P("grp", "seq"),
            P(),
            P("grp", "seq"),
            P("grp", "seq"),
            P("grp", "seq"),
            P("seq", "grp"),
            P("grp", None, None),
        ),
        out_specs=(P("grp", None, "seq"), P("grp", "seq", None)),
        check_vma=False,
    )
```

profile of v0, /device:TPU:0, one launch (start us, length us, event | category | flops | bytes accessed | tf_op | source)
XLA Modules:
  0.0 326.0 jit_solution(11023302746642176019)
XLA Ops:
  7.2 1.4 multiply_reduce_fusion.1
  8.6 1.3 reduce_max.9
  10.6 0.8 multiply_convert_fusion
  11.4 11.3 %all-gather.2 = bf16[8,9,2048]{2,1,0:T(8,128)(2,1)S(1)} all-gather(bf16[1,9,2048]{2,1,0:T(8,128)(2,1)S(1)} %pad_bitcast_fusion), channel_id=2, replica_groups=mesh['grp'=4,'seq'=8] {'seq'}, dimensions={0}, use_global_device_ids=true | all-gather | bytes 331776 | tf_op jit(solution)/shard_map/all_gather | solution.py:61
  22.7 0.2 fusion.39
  22.9 0.1 iota_compare_fusion.1
  23.0 0.2 reduce-window.9
  23.2 0.1 iota_add_fusion
  23.3 0.1 add.65
  23.4 0.1 lt.18
  23.4 0.2 convolution_convert_fusion.6
  23.6 0.1 broadcast_in_dim_reshape.9
  23.8 0.7 copy.18
  24.5 4.9 %all-to-all-start = ((bf16[1,48,4,512]{3,1,0,2:T(8,128)(2,1)}), bf16[1,48,4,512]{3,1,0,2:T(8,128)(2,1)S(1)}, u32[]{:S(2)}, u32[]{:S(2)}) async-start(bf16[1,48,4,512]{3,1,0,2:T(8,128)(2,1)} %copy.18), calls=%async_computation | async-start | bytes 393216 | tf_op jit(solution)/shard_map/all_to_all | solution.py:73
  29.4 1.5 copy.28
  30.9 0.8 dynamic-slice_reduce_fusion
  31.7 0.2 convolution_convert_fusion.10
  31.9 0.1 broadcast_in_dim_reshape.10
  31.9 0.7 copy.22
  32.6 4.8 %all-to-all-done = bf16[1,48,4,512]{3,1,0,2:T(8,128)(2,1)S(1)} async-done(((bf16[1,48,4,512]{3,1,0,2:T(8,128)(2,1)}), bf16[1,48,4,512]{3,1,0,2:T(8,128)(2,1)S(1)}, u32[]{:S(2)}, u32[]{:S(2)}) %all-to-all-start) | async-done | bytes 196640 | tf_op jit(solution)/shard_map/all_to_all | solution.py:73
  37.4 3.3 %all-to-all-start.1 = ((bf16[1,48,4,256]{3,1,0,2:T(8,128)(2,1)}), bf16[1,48,4,256]{3,1,0,2:T(8,128)(2,1)S(1)}, u32[]{:S(2)}, u32[]{:S(2)}) async-start(bf16[1,48,4,256]{3,1,0,2:T(8,128)(2,1)} %copy.22), calls=%async_computation.5 | async-start | bytes 196608 | tf_op jit(solution)/shard_map/all_to_all | solution.py:83
  40.7 0.0 reduce-scatter.8.cloned.1.call-start
  40.7 1.1 convolution_convert_fusion.7
  41.9 0.0 reduce-scatter.16.cloned.1.call-start
  41.9 4.5 %all-to-all-done.1 = bf16[1,48,4,256]{3,1,0,2:T(8,128)(2,1)S(1)} async-done(((bf16[1,48,4,256]{3,1,0,2:T(8,128)(2,1)}), bf16[1,48,4,256]{3,1,0,2:T(8,128)(2,1)S(1)}, u32[]{:S(2)}, u32[]{:S(2)}) %all-to-all-start.1) | async-done | bytes 98336 | tf_op jit(solution)/shard_map/all_to_all | solution.py:83
  46.5 11.9 %all_gather.32 = bf16[192,2048]{1,0:T(8,128)(2,1)S(1)} all-gather(bf16[192,256]{1,0:T(8,128)(2,1)S(1)} %bitcast.93), channel_id=1, replica_groups=mesh['grp'=4,'seq'=8] {'seq'}, dimensions={1}, use_global_device_ids=true | all-gather | bytes 884736 | tf_op jit(solution)/shard_map/all_gather | solution.py:86
  58.4 7.2 %convolution_convert_fusion = bf16[192,2048]{1,0:T(8,128)(2,1)} fusion(bf16[192,2048]{1,0:T(8,128)(2,1)S(1)} %all_gather.32, bf16[2048,2048]{1,0:T(8,128)(2,1)} %param.14), kind=kOutput, calls=%fused_computation.1 | convolution fusion | flops 1611005952 | bytes 9961472 | tf_op jit(solution)/shard_map/dot_general | solution.py:22
  65.7 1.6 collective-permute-start
  67.3 27.1 %all-gather.1 = bf16[384,1024]{1,0:T(8,128)(2,1)S(1)} all-gather(bf16[48,1024]{1,0:T(8,128)(2,1)S(1)} %collective-permute-done), channel_id=3, replica_groups=mesh['grp'=4,'seq'=8] {'seq'}, dimensions={0}, use_global_device_ids=true | all-gather | bytes 884736 | tf_op jit(solution)/shard_map/all_gather | solution.py:90
  94.4 0.8 copy.19
  95.3 0.2 copy.27
  95.5 6.1 %convolution_convert_fusion.3 = bf16[192,2048]{1,0:T(8,128)(2,1)} fusion(bf16[192,2048]{1,0:T(8,128)(2,1)S(1)} %bitcast.87, bf16[2048,2048]{1,0:T(8,128)(2,1)} %param.12), kind=kOutput, calls=%fused_computation.4 | convolution fusion | flops 1611005952 | bytes 9961472 | tf_op jit(solution)/shard_map/dot_general | solution.py:18
  101.6 0.0 reduce-scatter.12.cloned.1.call-start
  101.6 6.1 %convolution_convert_fusion.2 = bf16[192,2048]{1,0:T(8,128)(2,1)} fusion(bf16[192,2048]{1,0:T(8,128)(2,1)S(1)} %bitcast.88, bf16[2048,2048]{1,0:T(8,128)(2,1)} %param.13), kind=kOutput, calls=%fused_computation.3 | convolution fusion | flops 1611005952 | bytes 9961472 | tf_op jit(solution)/shard_map/dot_general | solution.py:18
  107.7 0.0 reduce-scatter.18.cloned.1.call-start
  107.8 14.5 %reduce-scatter.10.cloned.1.call-done = bf16[48,2048]{1,0:T(8,128)(2,1)} async-done(((bf16[192,2048]{1,0:T(8,128)(2,1)}), bf16[48,2048]{1,0:T(8,128)(2,1)}) %reduce-scatter.10.cloned.1.call-update) | async-done | bytes 196624 | tf_op jit(solution)/shard_map/reduce_scatter | solution.py:36
  122.3 24.9 %reduce-scatter.12.cloned.1.call-done = bf16[48,2048]{1,0:T(8,128)(2,1)} async-done(((bf16[192,2048]{1,0:T(8,128)(2,1)}), bf16[48,2048]{1,0:T(8,128)(2,1)}) %reduce-scatter.12.cloned.1.call-update) | async-done | bytes 196624 | tf_op jit(solution)/shard_map/reduce_scatter | solution.py:36
  147.1 1.4 fusion.8
  148.5 18.2 %all_gather.33 = bf16[192,2048]{1,0:T(8,128)(2,1)S(1)} all-gather(bf16[48,2048]{1,0:T(8,128)(2,1)S(1)} %get-tuple-element.3), channel_id=1, replica_groups=mesh['grp'=4,'seq'=8] {'grp'}, dimensions={0}, use_global_device_ids=true | all-gather | bytes 983040 | tf_op jit(solution)/shard_map/all_gather | solution.py:106
  166.7 6.3 %fusion.43 = f32[192,2048]{1,0:T(8,128)S(1)} fusion(bf16[192,2048]{1,0:T(8,128)(2,1)S(1)} %all_gather.33, bf16[2048,2048]{1,0:T(8,128)(2,1)} %param.12), kind=kOutput, calls=%fused_computation.73 | convolution fusion | flops 1610612736 | bytes 10747904 | tf_op jit(solution)/shard_map/dot_general | solution.py:22
  173.0 17.4 %all_gather.34 = bf16[192,2048]{1,0:T(8,128)(2,1)S(1)} all-gather(bf16[48,2048]{1,0:T(8,128)(2,1)S(1)} %get-tuple-element.2), channel_id=1, replica_groups=mesh['grp'=4,'seq'=8] {'grp'}, dimensions={0}, use_global_device_ids=true | all-gather | bytes 983040 | tf_op jit(solution)/shard_map/all_gather | solution.py:107
  190.4 6.3 %fusion = bf16[192,2048]{1,0:T(8,128)(2,1)S(1)} fusion(f32[192,2048]{1,0:T(8,128)S(1)} %fusion.43, bf16[192,2048]{1,0:T(8,128)(2,1)S(1)} %all_gather.34, bf16[2048,2048]{1,0:T(8,128)(2,1)} %param.13), kind=kOutput, calls=%fused_computation.5 | convolution fusion | flops 1611399168 | bytes 11534336 | tf_op jit(solution)/shard_map/dot_general | solution.py:22
  196.7 0.6 reshape.115
  197.2 1.1 copy.23
  198.4 0.0 reduce-scatter.14.cloned.1.call-start
  198.4 16.8 %all_gather.31 = bf16[192,2048]{1,0:T(8,128)(2,1)S(1)} all-gather(bf16[48,2048]{1,0:T(8,128)(2,1)S(1)} %get-tuple-element.4), channel_id=1, replica_groups=mesh['grp'=4,'seq'=8] {'grp'}, dimensions={0}, use_global_device_ids=true | all-gather | bytes 983040 | tf_op jit(solution)/shard_map/all_gather | solution.py:108
  215.2 18.1 %reduce-scatter.18.cloned.1.call-done = bf16[48,1024]{1,0:T(8,128)(2,1)} async-done(((bf16[384,1024]{1,0:T(8,128)(2,1)}), bf16[48,1024]{1,0:T(8,128)(2,1)}) %reduce-scatter.18.cloned.1.call-update) | async-done | bytes 98320 | tf_op jit(solution)/shard_map/reduce_scatter | solution.py:97
  233.4 1.5 collective-permute-start.2
  234.9 5.2 %convolution_convert_fusion.1 = bf16[192,2048]{1,0:T(8,128)(2,1)S(1)} fusion(bf16[192,2048]{1,0:T(8,128)(2,1)S(1)} %all_gather.31, bf16[2048,2048]{1,0:T(8,128)(2,1)} %param.14), kind=kOutput, calls=%fused_computation.2 | convolution fusion | flops 1611005952 | bytes 9961472 | tf_op jit(solution)/shard_map/dot_general | solution.py:18
  240.1 0.6 reshape.112
  240.7 1.1 copy.20
  241.8 0.0 reduce-scatter.20.cloned.1.call-start
  241.9 1.1 add_convert_fusion
  243.0 16.2 %all_gather.35 = bf16[192,1024]{1,0:T(8,128)(2,1)S(1)} all-gather(bf16[48,1024]{1,0:T(8,128)(2,1)S(1)} %add_convert_fusion), channel_id=1, replica_groups=mesh['grp'=4,'seq'=8] {'grp'}, dimensions={0}, use_global_device_ids=true | all-gather | bytes 491520 | tf_op jit(solution)/shard_map/all_gather | solution.py:116
  259.1 0.5 convolution_convert_fusion.8
  259.6 11.9 %all_to_all.45 = bf16[4,48,1,512]{3,1,2,0:T(8,128)(2,1)S(1)} all-to-all(bf16[4,48,1,512]{3,1,2,0:T(8,128)(2,1)S(1)} %bitcast.85), channel_id=1, replica_groups=mesh['grp'=4,'seq'=8] {'grp'}, dimensions={0} | all-to-all | bytes 393216 | tf_op jit(solution)/shard_map/all_to_all | solution.py:118
  271.5 0.2 copy.25
  271.7 1.0 convolution_convert_fusion.5
  272.7 6.1 %reduce-scatter.14.cloned.1.call-done = bf16[48,1024]{1,0:T(8,128)(2,1)} async-done(((bf16[384,1024]{1,0:T(8,128)(2,1)}), bf16[48,1024]{1,0:T(8,128)(2,1)}) %reduce-scatter.14.cloned.1.call-update) | async-done | bytes 98320 | tf_op jit(solution)/shard_map/reduce_scatter | solution.py:97
  278.8 1.5 collective-permute-start.1
  280.3 0.9 fusion.2
  281.2 35.1 %reduce-scatter.20.cloned.1.call-done = bf16[8,2048]{1,0:T(8,128)(2,1)} async-done(((bf16[64,2048]{1,0:T(8,128)(2,1)}), bf16[8,2048]{1,0:T(8,128)(2,1)}) %reduce-scatter.20.cloned.1.call-update) | async-done | bytes 32784 | tf_op jit(solution)/shard_map/reduce_scatter | solution.py:122
  316.3 0.9 multiply_reduce_fusion
  317.2 1.9 fusion.1
  (27 shorter events, 0.3 us)
Async XLA Ops:
  7.2 33.6 %copy-start = (bf16[512,1024]{1,0:T(8,128)(2,1)S(1)}, bf16[512,1024]{1,0:T(8,128)(2,1)}, u32[]{:S(2)}) copy-start(bf16[512,1024]{1,0:T(8,128)(2,1)} %param.11) | copy-start | bytes 3145732
  24.5 12.9 %all-to-all-start = ((bf16[1,48,4,512]{3,1,0,2:T(8,128)(2,1)}), bf16[1,48,4,512]{3,1,0,2:T(8,128)(2,1)S(1)}, u32[]{:S(2)}, u32[]{:S(2)}) async-start(bf16[1,48,4,512]{3,1,0,2:T(8,128)(2,1)} %copy.18), calls=%async_computation | async-start | bytes 393216 | tf_op jit(solution)/shard_map/all_to_all | solution.py:73
  37.4 9.1 %all-to-all-start.1 = ((bf16[1,48,4,256]{3,1,0,2:T(8,128)(2,1)}), bf16[1,48,4,256]{3,1,0,2:T(8,128)(2,1)S(1)}, u32[]{:S(2)}, u32[]{:S(2)}) async-start(bf16[1,48,4,256]{3,1,0,2:T(8,128)(2,1)} %copy.22), calls=%async_computation.5 | async-start | bytes 196608 | tf_op jit(solution)/shard_map/all_to_all | solution.py:83
  40.7 25.1 %reduce-scatter.8.cloned.1.call-start = ((), (), s32[]{:S(2)}) async-start(), calls=%async_computation.10 | async-start | bytes 491520 | tf_op jit(solution)/shard_map/reduce_scatter | solution.py:36
  41.9 65.9 %reduce-scatter.16.cloned.1.call-start = ((), (), s32[]{:S(2)}) async-start(), calls=%async_computation.14 | async-start | bytes 983040 | tf_op jit(solution)/shard_map/reduce_scatter | solution.py:36
  65.7 56.6 %reduce-scatter.10.cloned.1.call-start = ((), (), s32[]{:S(2)}) async-start(), calls=%async_computation.11 | async-start | bytes 983040 | tf_op jit(solution)/shard_map/reduce_scatter | solution.py:36
  65.7 1.6 collective-permute-start
  101.6 45.6 %reduce-scatter.12.cloned.1.call-start = ((), (), s32[]{:S(2)}) async-start(), calls=%async_computation.12 | async-start | bytes 983040 | tf_op jit(solution)/shard_map/reduce_scatter | solution.py:36
  107.7 125.6 %reduce-scatter.18.cloned.1.call-start = ((), (), s32[]{:S(2)}) async-start(), calls=%async_computation.15 | async-start | bytes 884736 | tf_op jit(solution)/shard_map/reduce_scatter | solution.py:97
  198.4 80.4 %reduce-scatter.14.cloned.1.call-start = ((), (), s32[]{:S(2)}) async-start(), calls=%async_computation.13 | async-start | bytes 884736 | tf_op jit(solution)/shard_map/reduce_scatter | solution.py:97
  215.2 65.1 %copy-start.1 = (bf16[48,1024]{1,0:T(8,128)(2,1)S(1)}, bf16[48,1024]{1,0:T(8,128)(2,1)}, u32[]{:S(2)}) copy-start(bf16[48,1024]{1,0:T(8,128)(2,1)} %reduce-scatter.8.cloned.1.call-done) | copy-start | bytes 294916
  233.4 8.5 %collective-permute-start.2 = (bf16[48,1024]{1,0:T(8,128)(2,1)}, bf16[48,1024]{1,0:T(8,128)(2,1)S(1)}, u32[]{:S(2)}, u32[]{:S(2)}) collective-permute-start(bf16[48,1024]{1,0:T(8,128)(2,1)} %reduce-scatter.18.cloned.1.call-done), channel_id=1, source_target_pairs={{0,0},{1,1},{2,8},{3,9},{4,16},{5,17},{6,24},{7,25},{8,2},{9,3},{1... | collective-permute-start | bytes 294920 | tf_op jit(solution)/shard_map/ppermute | solution.py:46
  240.1 76.2 %copy-start.2 = (f32[2048]{0:T(1024)S(1)}, f32[2048]{0:T(1024)}, u32[]{:S(2)}) copy-start(f32[2048]{0:T(1024)} %param.10) | copy-start | bytes 24580
  240.1 77.1 %copy-start.3 = (s32[1,128]{1,0:T(1,128)S(1)}, s32[1,128]{1,0:T(1,128)}, u32[]{:S(2)}) copy-start(s32[1,128]{1,0:T(1,128)} %param.9) | copy-start | bytes 1540
  241.8 74.5 %reduce-scatter.20.cloned.1.call-start = ((), (), s32[]{:S(2)}) async-start(), calls=%async_computation.16 | async-start | bytes 294912 | tf_op jit(solution)/shard_map/reduce_scatter | solution.py:122
  278.8 1.5 collective-permute-start.1
Sparse Core Ops, SparseCore 0:
  44.4 21.0 reduce-scatter.7
  67.8 26.4 reduce-scatter.15
  101.7 20.5 reduce-scatter.9
  124.5 22.5 reduce-scatter.11
  198.5 34.8 reduce-scatter.17
  242.0 36.7 reduce-scatter.13
  282.7 33.5 reduce-scatter.19
where the time goes:
time: 327 us; the launch traced here: 326 us
  blocking collectives  131 us (40%)
  waiting for transfers between devices  108 us (33%)
  matrix products  45.5 us (14%)
  between operations  15 us (5%)
  starting transfers between devices  13.1 us (4%)
  local copies, waits for them, and re-layouts  8.58 us (3%)
  other arithmetic  4.91 us (2%)
    reduce_scatter x4, waiting for transfers between devices, grp_total(): lax.psum_scatter(partial_value.astype(bf16), 'grp', scatter_dimension=0,...  39.4 us
    reduce_scatter x1, waiting for transfers between devices, shards(): lax.psum_scatter(term, 'seq', scatter_dimension=0, tiled=True).astype(f32)  35.1 us
    all_gather x1, blocking collectives, spread(): every = lax.all_gather(swap(cols), 'seq', axis=0)  27.1 us
    dot_general x11, matrix products, matmul(): return jnp.dot(a, b, preferred_element_type=f32)  25.2 us
    reduce_scatter x2, waiting for transfers between devices, column_total(): lax.psum_scatter(part, 'seq', scatter_dimension=0, tiled=True)  24.2 us
    dot_general x4, matrix products, matmul_t(): lax.dot_general(a, b, (((1,), (1,)), ((), ())), preferred_element_type=f32)  20.3 us
    all_gather x1, blocking collectives, shards(): grad_gate = lax.all_gather(grad_gate, 'grp', axis=0, tiled=True)  18.2 us
    all_gather x1, blocking collectives, shards(): grad_up = lax.all_gather(grad_up, 'grp', axis=0, tiled=True)  17.4 us
  transfers between devices with their start and end apart: 12, of which 7 were waited for; matrix products, arithmetic and copies ran while one was open for 11% of the time, Pallas kernels for 0%

commit v1 on v0

--- a/solution.py
+++ b/solution.py
@@ -2,6 +2,7 @@
 import jax.numpy as jnp
 from jax import lax
 from jax.sharding import PartitionSpec as P
+from jax.lax import all_gather
 
 SEG_CAP = 8
 norm_eps = 1e-06
@@ -104,8 +105,11 @@
         grad_gate = (grad_hidden * up_value * derivative).astype(bf16)
         grad_up = (grad_hidden * activated).astype(bf16)
         grad_gate = lax.all_gather(grad_gate, "grp", axis=0, tiled=True)
-        grad_up = lax.all_gather(grad_up, "grp", axis=0, tiled=True)
-        hidden = lax.all_gather(hidden, "grp", axis=0, tiled=True)
+        grad_up, hidden = jnp.split(
+            all_gather(jnp.concatenate([grad_up, hidden], axis=1), "grp", tiled=True, axis=0),
+            [grad_up.shape[1]],
+            axis=1,
+        )
         back_cols = column_total(matmul_t(grad_gate, w_gate) + matmul_t(grad_up, w_up))
         down_cols = column_total(matmul(hidden, w_down))
         out_cols = (x_cols.astype(f32) + down_cols).astype(bf16)

time: 327 us -> 329 us (level)
  blocking collectives: 131 us -> 102 us
  waiting for transfers between devices: 108 us -> 136 us
    all_gather x2 -> x0, blocking collectives: 34.2 us -> none  [the longest x1 17.4 us: shards(): grad_up = lax.all_gather(grad_up, 'grp', axis=0, tiled=True)]
    reduce_scatter x2, waiting for transfers between devices: 24.2 us -> 41.5 us  [column_total(): lax.psum_scatter(part, 'seq', scatter_dimension=0, tiled=True)]
    all_gather x0 -> x1, waiting for transfers between devices: none -> 10.3 us  [shards(): all_gather(jnp.concatenate([grad_up, hidden], axis=1), 'grp', tiled=True,...]
    all_gather x1, blocking collectives: 18.2 us -> 23.6 us  [shards(): grad_gate = lax.all_gather(grad_gate, 'grp', axis=0, tiled=True)]
  transfers between devices with their start and end apart: 12 -> 13, of which waited for: 7 -> 8; matrix products, arithmetic and copies ran while one was open for 11% -> 13% of each run, Pallas kernels for 0% -> 0%
where the time goes in v1:
time: 329 us; the launch traced here: 328 us
  waiting for transfers between devices  136 us (41%)
  blocking collectives  102 us (31%)
  matrix products  47.5 us (14%)
  between operations  15 us (5%)
  starting transfers between devices  13.1 us (4%)
  local copies, waits for them, and re-layouts  8.59 us (3%)
  other arithmetic  5.77 us (2%)
    reduce_scatter x2, waiting for transfers between devices, column_total(): lax.psum_scatter(part, 'seq', scatter_dimension=0, tiled=True)  41.5 us
    reduce_scatter x4, waiting for transfers between devices, grp_total(): lax.psum_scatter(partial_value.astype(bf16), 'grp', scatter_dimension=0,...  39.4 us
    reduce_scatter x1, waiting for transfers between devices, shards(): lax.psum_scatter(term, 'seq', scatter_dimension=0, tiled=True).astype(f32)  35.1 us
    all_gather x1, blocking collectives, spread(): every = lax.all_gather(swap(cols), 'seq', axis=0)  27.1 us
    dot_general x11, matrix products, matmul(): return jnp.dot(a, b, preferred_element_type=f32)  25.3 us
    all_gather x1, blocking collectives, shards(): grad_gate = lax.all_gather(grad_gate, 'grp', axis=0, tiled=True)  23.6 us
    dot_general x4, matrix products, matmul_t(): lax.dot_general(a, b, (((1,), (1,)), ((), ())), preferred_element_type=f32)  22.2 us
    all_gather x1, blocking collectives, shards(): grad_x = lax.all_gather(grad_x, 'grp', axis=0, tiled=True)  16.1 us
  transfers between devices with their start and end apart: 13, of which 8 were waited for; matrix products, arithmetic and copies ran while one was open for 13% of the time, Pallas kernels for 0%

profile of v1, /device:TPU:0, one launch (start us, length us, event | category | flops | bytes accessed | tf_op | source)
XLA Modules:
  0.0 327.7 jit_solution(10298362406757991626)
XLA Ops:
  7.2 1.4 reduce_max.9
  9.2 1.4 multiply_reduce_fusion.1
  10.6 0.8 multiply_convert_fusion
  11.4 11.3 %all-gather.2 = bf16[8,9,2048]{2,1,0:T(8,128)(2,1)S(1)} all-gather(bf16[1,9,2048]{2,1,0:T(8,128)(2,1)S(1)} %pad_bitcast_fusion), channel_id=2, replica_groups=mesh['grp'=4,'seq'=8] {'seq'}, dimensions={0}, use_global_device_ids=true | all-gather | bytes 331776 | tf_op jit(solution)/shard_map/all_gather | solution.py:62
  22.7 0.2 fusion.41
  22.9 0.1 iota_compare_fusion.1
  23.0 0.2 reduce-window.9
  23.2 0.1 lt.18
  23.3 0.1 iota_add_fusion
  23.4 0.1 add.65
  23.4 0.2 convolution_convert_fusion.6
  23.6 0.1 broadcast_in_dim_reshape.9
  23.8 0.7 copy.18
  24.5 4.9 %all-to-all-start = ((bf16[1,48,4,512]{3,1,0,2:T(8,128)(2,1)}), bf16[1,48,4,512]{3,1,0,2:T(8,128)(2,1)S(1)}, u32[]{:S(2)}, u32[]{:S(2)}) async-start(bf16[1,48,4,512]{3,1,0,2:T(8,128)(2,1)} %copy.18), calls=%async_computation | async-start | bytes 393216 | tf_op jit(solution)/shard_map/all_to_all | solution.py:74
  29.4 1.5 copy.27
  30.9 0.8 dynamic-slice_reduce_fusion
  31.7 0.2 convolution_convert_fusion.10
  31.9 0.1 broadcast_in_dim_reshape.10
  31.9 0.7 copy.20
  32.6 4.8 %all-to-all-done = bf16[1,48,4,512]{3,1,0,2:T(8,128)(2,1)S(1)} async-done(((bf16[1,48,4,512]{3,1,0,2:T(8,128)(2,1)}), bf16[1,48,4,512]{3,1,0,2:T(8,128)(2,1)S(1)}, u32[]{:S(2)}, u32[]{:S(2)}) %all-to-all-start) | async-done | bytes 196640 | tf_op jit(solution)/shard_map/all_to_all | solution.py:74
  37.4 3.3 %all-to-all-start.1 = ((bf16[1,48,4,256]{3,1,0,2:T(8,128)(2,1)}), bf16[1,48,4,256]{3,1,0,2:T(8,128)(2,1)S(1)}, u32[]{:S(2)}, u32[]{:S(2)}) async-start(bf16[1,48,4,256]{3,1,0,2:T(8,128)(2,1)} %copy.20), calls=%async_computation.2 | async-start | bytes 196608 | tf_op jit(solution)/shard_map/all_to_all | solution.py:84
  40.7 0.0 reduce-scatter.8.cloned.1.call-start
  40.7 1.1 convolution_convert_fusion.7
  41.9 0.0 reduce-scatter.10.cloned.1.call-start
  41.9 4.5 %all-to-all-done.1 = bf16[1,48,4,256]{3,1,0,2:T(8,128)(2,1)S(1)} async-done(((bf16[1,48,4,256]{3,1,0,2:T(8,128)(2,1)}), bf16[1,48,4,256]{3,1,0,2:T(8,128)(2,1)S(1)}, u32[]{:S(2)}, u32[]{:S(2)}) %all-to-all-start.1) | async-done | bytes 98336 | tf_op jit(solution)/shard_map/all_to_all | solution.py:84
  46.5 11.9 %all_gather.26 = bf16[192,2048]{1,0:T(8,128)(2,1)S(1)} all-gather(bf16[192,256]{1,0:T(8,128)(2,1)S(1)} %bitcast.91), channel_id=1, replica_groups=mesh['grp'=4,'seq'=8] {'seq'}, dimensions={1}, use_global_device_ids=true | all-gather | bytes 884736 | tf_op jit(solution)/shard_map/all_gather | solution.py:87
  58.4 7.2 %convolution_convert_fusion.3 = bf16[192,2048]{1,0:T(8,128)(2,1)} fusion(bf16[192,2048]{1,0:T(8,128)(2,1)S(1)} %all_gather.26, bf16[2048,2048]{1,0:T(8,128)(2,1)} %param.14), kind=kOutput, calls=%fused_computation.4 | convolution fusion | flops 1611005952 | bytes 9961472 | tf_op jit(solution)/shard_map/dot_general | solution.py:23
  65.7 1.6 collective-permute-start
  67.3 27.1 %all-gather.1 = bf16[384,1024]{1,0:T(8,128)(2,1)S(1)} all-gather(bf16[48,1024]{1,0:T(8,128)(2,1)S(1)} %collective-permute-done), channel_id=3, replica_groups=mesh['grp'=4,'seq'=8] {'seq'}, dimensions={0}, use_global_device_ids=true | all-gather | bytes 884736 | tf_op jit(solution)/shard_map/all_gather | solution.py:91
  94.4 0.8 copy.21
  95.2 0.2 copy.29
  95.5 6.1 %convolution_convert_fusion.2 = bf16[192,2048]{1,0:T(8,128)(2,1)} fusion(bf16[192,2048]{1,0:T(8,128)(2,1)S(1)} %bitcast.85, bf16[2048,2048]{1,0:T(8,128)(2,1)} %param.12), kind=kOutput, calls=%fused_computation.3 | convolution fusion | flops 1611005952 | bytes 9961472 | tf_op jit(solution)/shard_map/dot_general | solution.py:19
  101.6 0.0 reduce-scatter.14.cloned.1.call-start
  101.6 6.1 %convolution_convert_fusion.1 = bf16[192,2048]{1,0:T(8,128)(2,1)} fusion(bf16[192,2048]{1,0:T(8,128)(2,1)S(1)} %bitcast.86, bf16[2048,2048]{1,0:T(8,128)(2,1)} %param.13), kind=kOutput, calls=%fused_computation.2 | convolution fusion | flops 1611005952 | bytes 9961472 | tf_op jit(solution)/shard_map/dot_general | solution.py:19
  107.7 0.0 all-gather.5.cloned.1.call-start
  107.8 14.5 %reduce-scatter.12.cloned.1.call-done = bf16[48,2048]{1,0:T(8,128)(2,1)} async-done(((bf16[192,2048]{1,0:T(8,128)(2,1)}), bf16[48,2048]{1,0:T(8,128)(2,1)}) %reduce-scatter.12.cloned.1.call-update) | async-done | bytes 196624 | tf_op jit(solution)/shard_map/reduce_scatter | solution.py:37
  122.3 24.9 %reduce-scatter.14.cloned.1.call-done = bf16[48,2048]{1,0:T(8,128)(2,1)} async-done(((bf16[192,2048]{1,0:T(8,128)(2,1)}), bf16[48,2048]{1,0:T(8,128)(2,1)}) %reduce-scatter.14.cloned.1.call-update) | async-done | bytes 196624 | tf_op jit(solution)/shard_map/reduce_scatter | solution.py:37
  147.2 1.4 fusion.10
  148.5 0.8 pad_maximum_fusion
  149.3 0.0 reduce-scatter.18.cloned.1.call-start
  149.4 23.6 %all_gather.30 = bf16[192,2048]{1,0:T(8,128)(2,1)S(1)} all-gather(bf16[48,2048]{1,0:T(8,128)(2,1)S(1)} %get-tuple-element.2), channel_id=1, replica_groups=mesh['grp'=4,'seq'=8] {'grp'}, dimensions={0}, use_global_device_ids=true | all-gather | bytes 983040 | tf_op jit(solution)/shard_map/all_gather | solution.py:107
  172.9 7.5 %fusion.45 = f32[192,2048]{1,0:T(8,128)} fusion(bf16[192,2048]{1,0:T(8,128)(2,1)S(1)} %all_gather.30, bf16[2048,2048]{1,0:T(8,128)(2,1)} %param.12), kind=kOutput, calls=%fused_computation.76 | convolution fusion | flops 1610612736 | bytes 10747904 | tf_op jit(solution)/shard_map/dot_general | solution.py:23
  180.4 10.3 %all-gather.5.cloned.1.call-done = bf16[192,4096]{1,0:T(8,128)(2,1)} async-done(((bf16[48,4096]{1,0:T(8,128)(2,1)}), bf16[192,4096]{1,0:T(8,128)(2,1)}) %all-gather.5.cloned.1.call-update) | async-done | bytes 1572880 | tf_op jit(solution)/shard_map/all_gather | solution.py:109
  190.7 6.9 %fusion = bf16[192,2048]{1,0:T(8,128)(2,1)S(1)} fusion(f32[192,2048]{1,0:T(8,128)} %fusion.45, bf16[2048,2048]{1,0:T(8,128)(2,1)} %param.13, bf16[192,4096]{1,0:T(8,128)(2,1)} %all-gather.5.cloned.1.call-done), kind=kOutput, calls=%fused_computation.5 | convolution fusion | flops 1611399168 | bytes 11534336 | tf_op jit(solution)/shard_map/dot_general | solution.py:23
  197.7 0.6 reshape.115
  198.2 1.1 copy.23
  199.4 35.4 %reduce-scatter.18.cloned.1.call-done = bf16[48,1024]{1,0:T(8,128)(2,1)} async-done(((bf16[384,1024]{1,0:T(8,128)(2,1)}), bf16[48,1024]{1,0:T(8,128)(2,1)}) %reduce-scatter.18.cloned.1.call-update) | async-done | bytes 98320 | tf_op jit(solution)/shard_map/reduce_scatter | solution.py:98
  234.8 1.5 collective-permute-start.2
  236.4 5.4 %convolution_convert_fusion = bf16[192,2048]{1,0:T(8,128)(2,1)S(1)} fusion(bf16[2048,2048]{1,0:T(8,128)(2,1)} %param.14, bf16[192,4096]{1,0:T(8,128)(2,1)} %all-gather.5.cloned.1.call-done), kind=kOutput, calls=%fused_computation.1 | convolution fusion | flops 1611005952 | bytes 9961472 | tf_op jit(solution)/shard_map/dot_general | solution.py:19
  241.8 0.6 reshape.113
  242.4 1.1 copy.22
  243.5 0.0 reduce-scatter.20.cloned.1.call-start
  243.6 1.1 add_convert_fusion
  244.7 16.1 %all_gather.31 = bf16[192,1024]{1,0:T(8,128)(2,1)S(1)} all-gather(bf16[48,1024]{1,0:T(8,128)(2,1)S(1)} %add_convert_fusion), channel_id=1, replica_groups=mesh['grp'=4,'seq'=8] {'grp'}, dimensions={0}, use_global_device_ids=true | all-gather | bytes 491520 | tf_op jit(solution)/shard_map/all_gather | solution.py:120
  260.8 0.5 convolution_convert_fusion.8
  261.3 11.9 %all_to_all.45 = bf16[4,48,1,512]{3,1,2,0:T(8,128)(2,1)S(1)} all-to-all(bf16[4,48,1,512]{3,1,2,0:T(8,128)(2,1)S(1)} %bitcast.83), channel_id=1, replica_groups=mesh['grp'=4,'seq'=8] {'grp'}, dimensions={0} | all-to-all | bytes 393216 | tf_op jit(solution)/shard_map/all_to_all | solution.py:122
  273.2 0.2 copy.25
  273.4 1.0 convolution_convert_fusion.5
  274.4 6.1 %reduce-scatter.16.cloned.1.call-done = bf16[48,1024]{1,0:T(8,128)(2,1)} async-done(((bf16[384,1024]{1,0:T(8,128)(2,1)}), bf16[48,1024]{1,0:T(8,128)(2,1)}) %reduce-scatter.16.cloned.1.call-update) | async-done | bytes 98320 | tf_op jit(solution)/shard_map/reduce_scatter | solution.py:98
  280.5 1.5 collective-permute-start.1
  282.0 0.9 fusion.2
  282.9 35.1 %reduce-scatter.20.cloned.1.call-done = bf16[8,2048]{1,0:T(8,128)(2,1)} async-done(((bf16[64,2048]{1,0:T(8,128)(2,1)}), bf16[8,2048]{1,0:T(8,128)(2,1)}) %reduce-scatter.20.cloned.1.call-update) | async-done | bytes 32784 | tf_op jit(solution)/shard_map/reduce_scatter | solution.py:126
  318.0 0.9 multiply_reduce_fusion
  318.9 1.9 fusion.1
  (29 shorter events, 0.4 us)
Async XLA Ops:
  7.2 33.6 %copy-start = (bf16[512,1024]{1,0:T(8,128)(2,1)S(1)}, bf16[512,1024]{1,0:T(8,128)(2,1)}, u32[]{:S(2)}) copy-start(bf16[512,1024]{1,0:T(8,128)(2,1)} %param.11) | copy-start | bytes 3145732
  24.5 12.9 %all-to-all-start = ((bf16[1,48,4,512]{3,1,0,2:T(8,128)(2,1)}), bf16[1,48,4,512]{3,1,0,2:T(8,128)(2,1)S(1)}, u32[]{:S(2)}, u32[]{:S(2)}) async-start(bf16[1,48,4,512]{3,1,0,2:T(8,128)(2,1)} %copy.18), calls=%async_computation | async-start | bytes 393216 | tf_op jit(solution)/shard_map/all_to_all | solution.py:74
  37.4 9.1 %all-to-all-start.1 = ((bf16[1,48,4,256]{3,1,0,2:T(8,128)(2,1)}), bf16[1,48,4,256]{3,1,0,2:T(8,128)(2,1)S(1)}, u32[]{:S(2)}, u32[]{:S(2)}) async-start(bf16[1,48,4,256]{3,1,0,2:T(8,128)(2,1)} %copy.20), calls=%async_computation.2 | async-start | bytes 196608 | tf_op jit(solution)/shard_map/all_to_all | solution.py:84
  40.7 25.1 %reduce-scatter.8.cloned.1.call-start = ((), (), s32[]{:S(2)}) async-start(), calls=%async_computation.10 | async-start | bytes 491520 | tf_op jit(solution)/shard_map/reduce_scatter | solution.py:37
  41.9 65.9 %reduce-scatter.10.cloned.1.call-start = ((), (), s32[]{:S(2)}) async-start(), calls=%async_computation.11 | async-start | bytes 983040 | tf_op jit(solution)/shard_map/reduce_scatter | solution.py:37
  65.7 56.6 %reduce-scatter.12.cloned.1.call-start = ((), (), s32[]{:S(2)}) async-start(), calls=%async_computation.12 | async-start | bytes 983040 | tf_op jit(solution)/shard_map/reduce_scatter | solution.py:37
  65.7 1.6 collective-permute-start
  101.6 45.6 %reduce-scatter.14.cloned.1.call-start = ((), (), s32[]{:S(2)}) async-start(), calls=%async_computation.13 | async-start | bytes 983040 | tf_op jit(solution)/shard_map/reduce_scatter | solution.py:37
  107.7 83.0 %all-gather.5.cloned.1.call-start = ((), (), s32[]{:S(2)}) async-start(), calls=%async_computation.14 | async-start | bytes 1966080 | tf_op jit(solution)/shard_map/all_gather | solution.py:109
  149.3 85.5 %reduce-scatter.18.cloned.1.call-start = ((), (), s32[]{:S(2)}) async-start(), calls=%async_computation.16 | async-start | bytes 884736 | tf_op jit(solution)/shard_map/reduce_scatter | solution.py:98
  199.4 82.7 %copy-start.1 = (bf16[48,1024]{1,0:T(8,128)(2,1)S(1)}, bf16[48,1024]{1,0:T(8,128)(2,1)}, u32[]{:S(2)}) copy-start(bf16[48,1024]{1,0:T(8,128)(2,1)} %reduce-scatter.8.cloned.1.call-done) | copy-start | bytes 294916
  199.4 81.1 %reduce-scatter.16.cloned.1.call-start = ((), (), s32[]{:S(2)}) async-start(), calls=%async_computation.15 | async-start | bytes 884736 | tf_op jit(solution)/shard_map/reduce_scatter | solution.py:98
  234.8 8.8 %collective-permute-start.2 = (bf16[48,1024]{1,0:T(8,128)(2,1)}, bf16[48,1024]{1,0:T(8,128)(2,1)S(1)}, u32[]{:S(2)}, u32[]{:S(2)}) collective-permute-start(bf16[48,1024]{1,0:T(8,128)(2,1)} %reduce-scatter.18.cloned.1.call-done), channel_id=1, source_target_pairs={{0,0},{1,1},{2,8},{3,9},{4,16},{5,17},{6,24},{7,25},{8,2},{9,3},{1... | collective-permute-start | bytes 294920 | tf_op jit(solution)/shard_map/ppermute | solution.py:47
  241.8 76.2 %copy-start.2 = (f32[2048]{0:T(1024)S(1)}, f32[2048]{0:T(1024)}, u32[]{:S(2)}) copy-start(f32[2048]{0:T(1024)} %param.10) | copy-start | bytes 24580
  241.8 77.1 %copy-start.3 = (s32[1,128]{1,0:T(1,128)S(1)}, s32[1,128]{1,0:T(1,128)}, u32[]{:S(2)}) copy-start(s32[1,128]{1,0:T(1,128)} %param.9) | copy-start | bytes 1540
  243.5 74.5 %reduce-scatter.20.cloned.1.call-start = ((), (), s32[]{:S(2)}) async-start(), calls=%async_computation.17 | async-start | bytes 294912 | tf_op jit(solution)/shard_map/reduce_scatter | solution.py:126
  280.5 1.5 collective-permute-start.1
Sparse Core Ops, SparseCore 0:
  44.4 21.0 reduce-scatter.7
  67.8 26.4 reduce-scatter.9
  101.7 20.5 reduce-scatter.11
  124.6 22.5 reduce-scatter.13
  149.4 41.2 all-gather.4
  199.5 35.3 reduce-scatter.17
  243.7 36.7 reduce-scatter.15
  284.4 33.5 reduce-scatter.19
